TPU v7x, 32 devices: a whole 2x2x4 slice. The times are simulated.
32 devices in a mesh: freq: 4 (over y, x), tile: 8 (over z, core).
Axes of the slice: x: 2, y: 2, z: 4, core: 2. Of those that a mesh axis runs over, the one named last changes fastest.
Arguments:
- traces: bfloat16 [256, 8192, 128], P('freq', 'tile'), may hold values from -6 to 6
- right_basis: bfloat16 [16, 8192, 4096], P('freq', 'tile'), may hold values from -0.25 to 0.25
- left_basis: bfloat16 [16, 8192, 4096], P('freq', 'tile'), may hold values from -0.09375 to 0.09375
- tile_ranks: int32 [16, 32, 32], P('freq'), may hold values from 8 to 64, as said below
Outputs:
- wavefield: bfloat16 [16, 2, 8192, 128], P('freq', None, 'tile')
Inputs may be any that keep to these rules, and one draw needn't show every extreme that they name: `tile_ranks`: diagonal tiles have rank 64; the ranks of the other tiles are drawn independently of the tile's position, evenly over the whole range.
All inputs are finite; a program needn't handle non-finite values.
Results may differ from a plain program's by a relative error of at most 0.015.
Values may be sent and summed in bfloat16 or wider, within the bound.
A program may use at most 320 MiB of HBM per device.

v0:
```python
import math

import jax
import jax.numpy as jnp
from jax import lax
from jax.sharding import PartitionSpec as P

N = 8192
TB = 256
R = 64


def twiddles(freq_ids, time_ids, total_time):
    phase_int = freq_ids[:, None] * time_ids[None, :] % total_time
    angle_rad = phase_int.astype(jnp.float32) * (2.0 * math.pi / total_time)
    factor = 1.0 / math.sqrt(total_time)
    return jnp.stack([jnp.cos(angle_rad) * factor, -jnp.sin(angle_rad) * factor], 1).astype(
        jnp.bfloat16
    )


def send_pieces(rank_rows, tile_count, tile_rows, per_tile):
    freq_dev = rank_rows.shape[1]
    rank_max = rank_rows.shape[4]
    sources = rank_rows.shape[5]
    if tile_rows < tile_count:
        copies = tile_count // tile_rows
        outgoing = jnp.broadcast_to(rank_rows[:, None], (tile_rows, copies) + rank_rows.shape[1:])
        outgoing = outgoing.reshape((tile_count,) + rank_rows.shape[1:])
    else:
        outgoing = rank_rows
    received = lax.all_to_all(outgoing, "tile", split_axis=0, concat_axis=2, tiled=True)
    row_tiles = received.shape[0]
    grouped = received.reshape(row_tiles, freq_dev, tile_rows, per_tile, 2, rank_max, sources)
    return jnp.sum(grouped.astype(jnp.float32), axis=3).astype(jnp.bfloat16)


def body(traces, right_basis, left_basis, tile_ranks):
    freq_count = lax.axis_size("freq")
    tile_count = lax.axis_size("tile")
    time_rows, grid_rows, sources = traces.shape
    freq_dev = right_basis.shape[0]
    total_time = time_rows * freq_count
    tile_rows = N // TB
    freq_ids = jnp.int32(0) + 1 + jnp.arange(lax.axis_size("freq") * freq_dev, dtype=jnp.int32)
    time_ids = lax.axis_index("freq") * time_rows + jnp.arange(time_rows, dtype=jnp.int32)
    twiddle = twiddles(freq_ids, time_ids, total_time)
    spectra = lax.psum_scatter(
        jnp.einsum("fpt,tns->fpns", twiddle, traces, preferred_element_type=jnp.float32).astype(
            jnp.bfloat16
        ),
        "freq",
        scatter_dimension=0,
        tiled=True,
    )
    piece_rows = min(TB, grid_rows)
    pieces_dev = grid_rows // piece_rows
    per_tile = max(TB // grid_rows, 1)
    spectra_pieces = spectra.reshape(freq_dev, 2, pieces_dev, piece_rows, sources)
    right_pieces = right_basis.reshape(freq_dev, pieces_dev, piece_rows, 2 * tile_rows * R)
    products = jnp.einsum(
        "fqnc,fpqns->cfqps", right_pieces, spectra_pieces, preferred_element_type=jnp.float32
    )
    products = products.reshape(2, tile_rows, R, freq_dev, pieces_dev, 2, sources)
    real_part = products[0, :, :, :, :, 0] - products[1, :, :, :, :, 1]
    imag_part = products[0, :, :, :, :, 1] + products[1, :, :, :, :, 0]
    stacked = jnp.transpose(jnp.stack([real_part, imag_part], 0), (1, 3, 4, 0, 2, 5))
    column_ids = (
        lax.axis_index("tile") * pieces_dev + jnp.arange(pieces_dev, dtype=jnp.int32)
    ) // per_tile
    onehot = (column_ids[:, None] == jnp.arange(tile_rows, dtype=jnp.int32)[None, :]).astype(
        jnp.int32
    )
    chosen = jnp.sum(tile_ranks[:, :, None, :] * onehot[None, None], axis=-1)
    keep_rows = jnp.arange(R, dtype=jnp.int32)[None, None, None, :] < chosen[..., None]
    keep_rows = jnp.transpose(keep_rows, (1, 0, 2, 3))[:, :, :, None, :, None]
    rank_rows = jnp.where(keep_rows, stacked, jnp.float32(0.0)).astype(jnp.bfloat16)
    coupled = send_pieces(rank_rows, tile_count, tile_rows, per_tile)
    row_tiles = coupled.shape[0]
    rows_tile = grid_rows // row_tiles
    real_coupled = coupled[:, :, :, 0]
    imag_coupled = coupled[:, :, :, 1]
    upper_half = jnp.stack([real_coupled, imag_coupled], -2)
    lower_half = jnp.stack([-imag_coupled, real_coupled], -2)
    operand = jnp.stack([upper_half, lower_half], 2)
    left_tiles = left_basis.reshape(freq_dev, row_tiles, rows_tile, 2, tile_rows, R)
    field_out = jnp.einsum(
        "frtajk,rfajkys->fyrts", left_tiles, operand, preferred_element_type=jnp.float32
    )
    return field_out.reshape(freq_dev, 2, grid_rows, sources).astype(jnp.bfloat16)


def solution(mesh):
    return jax.shard_map(
        body,
        mesh=mesh,
        in_specs=(
            P("freq", "tile", None),
            P("freq", "tile", None),
            P("freq", "tile", None),
            P("freq", None, None),
        ),
        out_specs=P("freq", None, "tile", None),
        check_vma=False,
    )
```

profile of v0, /device:TPU:0, one launch (start us, length us, event | category | flops | bytes accessed | tf_op | source)
XLA Modules:
  0.0 736.0 jit_solution(3858141168752758460)
XLA Ops:
  6.5 0.0 reduce-scatter.2.cloned.1.call-start
  6.5 0.1 multiply_convert_fusion.1
  6.7 21.0 %fusion.13 = bf16[16,2,1024,128]{3,0,2,1:T(8,128)(2,1)} fusion(bf16[64,1024,128]{2,1,0:T(8,128)(2,1)} %param.4, bf16[16,1,64]{2,0,1:T(8,128)(2,1)S(1)} %get-tuple-element.10, bf16[16,1,64]{2,0,1:T(8,128)(2,1)S(1)} %get-tuple-element.9), kind=kOutput, calls=%fused_computation.22 | convolution fusion | flops 541073408 | bytes 25169920 | tf_op jit(solution)/shard_map/fpt,tns->fpns/dot_general | solution.py:49
  27.7 0.0 copy-start.1
  27.7 9.0 %copy.35 = bf16[16,2,1024,128]{3,2,1,0:T(8,128)(2,1)} copy(bf16[16,2,1024,128]{3,0,2,1:T(8,128)(2,1)} %fusion.13) | data formatting | bytes 16777216 | tf_op jit(solution)/shard_map/convert_element_type | solution.py:49
  36.7 0.0 reduce-scatter.2.cloned.1.call-update
  36.7 0.1 fusion.31
  36.8 0.0 copy-done.1
  36.8 0.4 multiply_reduce_fusion
  37.1 0.1 iota_compare_fusion
  37.3 88.6 %reduce-scatter.2.cloned.1.call-done = bf16[4,2,1024,128]{3,2,1,0:T(8,128)(2,1)} async-done(((bf16[16,2,1024,128]{3,2,1,0:T(8,128)(2,1)}), bf16[4,2,1024,128]{3,2,1,0:T(8,128)(2,1)}) %reduce-scatter.2.cloned.1.call-update) | async-done | bytes 2097168 | tf_op jit(solution)/shard_map/reduce_scatter | solution.py:48
  125.9 33.9 %convolution_bitcast_fusion = f32[4096,4,4,2,128]{0,4,3,2,1:T(8,128)} fusion(bf16[4,4,256,4096,1]{3,2,4,1,0:T(8,128)(2,1)} %bitcast.71, bf16[4,2,4,256,128]{4,3,2,1,0:T(8,128)(2,1)} %bitcast.72), kind=kOutput, calls=%fused_computation.2 | convolution fusion | flops 8589934592 | bytes 102760448 | tf_op jit(solution)/shard_map/fqnc,fpqns->cfqps/dot_general | solution.py:61
  159.8 61.1 %copy.37 = f32[4096,4,4,2,128]{4,0,3,2,1:T(8,128)} copy(f32[4096,4,4,2,128]{0,4,3,2,1:T(8,128)} %convolution_bitcast_fusion) | data formatting | bytes 134217728 | tf_op jit(solution)/shard_map/fqnc,fpqns->cfqps/transpose | solution.py:61
  220.8 11.9 %fusion.7 = bf16[1,32,64,4,4,128]{5,2,1,4,3,0:T(8,128)(2,1)S(1)} fusion(f32[2,32,64,4,4,2,128]{6,2,1,0,5,4,3:T(8,128)} %bitcast.9), kind=kLoop, calls=%fused_computation.10 | loop fusion | flops 8388608 | bytes 41943040 | tf_op jit(solution)/shard_map/add | solution.py:66
  232.8 15.2 %fusion.9 = bf16[1,32,64,4,4,128]{5,2,1,4,3,0:T(8,128)(2,1)} fusion(f32[2,32,64,4,4,2,128]{6,2,1,0,5,4,3:T(8,128)} %bitcast.9), kind=kLoop, calls=%fused_computation.13 | loop fusion | flops 8388608 | bytes 41943040 | tf_op jit(solution)/shard_map/sub | solution.py:65
  248.0 8.2 %fusion.3 = bf16[32,4,4,2,64,128]{5,4,0,2,1,3:T(8,128)(2,1)S(1)} fusion(bf16[1,32,64,4,4,128]{5,2,1,4,3,0:T(8,128)(2,1)S(1)} %fusion.7, bf16[1,32,64,4,4,128]{5,2,1,4,3,0:T(8,128)(2,1)} %fusion.9, pred[32,4,4,64]{3,0,2,1:T(8,128)(4,1)S(1)} %iota_compare_fusion), kind=kLoop, calls=%fused_computation.5 | loop fusion | flops 41943040 | bytes 33587200 | tf_op jit(solution)/shard_map/convert_element_type | solution.py:77
  256.1 7.0 copy.40
  263.1 5.9 all-to-all-start
  269.1 90.5 %reshape.247 = bf16[4,4,256,2,32,64]{5,4,3,2,1,0:T(8,128)(2,1)} reshape(bf16[4,1024,4096]{2,1,0:T(8,128)(2,1)} %param.6) | data formatting | bytes 67108864 | tf_op jit(solution)/shard_map/reshape | solution.py:86
  359.6 272.9 %all-to-all-done = bf16[32,4,4,2,64,128]{5,4,2,1,3,0:T(8,128)(2,1)} async-done(((bf16[32,4,4,2,64,128]{5,4,2,1,3,0:T(8,128)(2,1)}), bf16[32,4,4,2,64,128]{5,4,2,1,3,0:T(8,128)(2,1)}, u32[]{:S(2)}, u32[]{:S(2)}) %all-to-all-start) | async-done | bytes 16777248 | tf_op jit(solution)/shard_map/all_to_all | solution.py:32
  632.5 8.4 %copy.41 = bf16[8,4,4,4,2,64,128]{6,5,3,0,1,2,4:T(8,128)(2,1)S(1)} copy(bf16[8,4,4,4,2,64,128]{6,5,3,2,4,1,0:T(8,128)(2,1)} %bitcast.13) | data formatting | bytes 33554432 | tf_op jit(solution)/shard_map/all_to_all | solution.py:32
  640.9 0.0 copy-start
  640.9 5.8 copy-done
  646.7 7.3 slice_bitcast_fusion.2
  654.0 7.8 %fusion.34 = bf16[4,4,32,64,1,128]{5,3,2,4,0,1:T(8,128)(2,1)} fusion(bf16[4,4,32,2,64,128]{5,4,2,0,1,3:T(8,128)(2,1)} %bitcast.70), kind=kLoop, calls=%fused_computation.48 | loop fusion | flops 4194304 | bytes 16777216 | tf_op jit(solution)/shard_map/neg | solution.py:84
  661.8 24.7 %maximum_bitcast_fusion.1 = (bf16[4,4,1,32,64,2,128]{6,4,3,2,5,0,1:T(8,128)(2,1)}, bf16[4,4,1,32,64,2,128]{6,4,3,2,5,0,1:T(8,128)(2,1)}) fusion(bf16[4,4,32,64,1,128]{5,3,2,4,0,1:T(8,128)(2,1)} %get-tuple-element.5, bf16[4,4,32,64,1,128]{5,3,2,4,0,1:T(8,128)(2,1)} %get-tuple-element.6, bf16[4,4,32,64,1,128]{5,3,2,4,0,1:T(8,128)(2,1)} %fusion.34), kind=kLoop, calls=%fused_computation.15 | loop fusion | flops 16777216 | bytes 58720256 | tf_op jit(solution)/shard_map/stack | solution.py:85
  686.5 40.3 %fusion.21 = bf16[4,2,4,256,128]{3,4,1,2,0:T(8,128)(2,1)S(1)} fusion(bf16[4,4,256,2,32,64,1]{5,4,3,2,1,0,6:T(8,128)(2,1)} %bitcast.22, bf16[4,4,1,32,64,2,128]{6,4,3,2,5,0,1:T(8,128)(2,1)} %get-tuple-element.8, bf16[4,4,1,32,64,2,128]{6,4,3,2,5,0,1:T(8,128)(2,1)} %get-tuple-element.7), kind=kOutput, calls=%fused_computation.25 | convolution fusion | flops 8607760384 | bytes 69206016 | tf_op jit(solution)/shard_map/frtajk,rfajkys->fyrts/dot_general | solution.py:87
  726.8 2.3 copy.45
  (3 shorter events, 0.0 us)
Async XLA Ops:
  6.5 119.3 %reduce-scatter.2.cloned.1.call-start = ((), (), s32[]{:S(2)}) async-start(), calls=%async_computation.2 | async-start | bytes 10485760 | tf_op jit(solution)/shard_map/reduce_scatter | solution.py:48
  27.7 9.1 %copy-start.1 = (s32[4,32,32]{2,1,0:T(8,128)S(1)}, s32[4,32,32]{2,1,0:T(8,128)}, u32[]{:S(2)}) copy-start(s32[4,32,32]{2,1,0:T(8,128)} %param.7) | copy-start | bytes 49156
  263.1 369.4 %all-to-all-start = ((bf16[32,4,4,2,64,128]{5,4,2,1,3,0:T(8,128)(2,1)}), bf16[32,4,4,2,64,128]{5,4,2,1,3,0:T(8,128)(2,1)}, u32[]{:S(2)}, u32[]{:S(2)}) async-start(bf16[32,4,4,2,64,128]{5,4,2,1,3,0:T(8,128)(2,1)} %copy.40), calls=%async_computation.1 | async-start | bytes 33554432 | tf_op jit(solution)/shard_map/all_to_all | solution.py:32
  640.9 5.8 copy-start
Sparse Core Ops, SparseCore 0:
  36.8 89.0 reduce-scatter.1
where the time goes:
time: 739 us; the launch traced here: 736 us
  waiting for transfers between devices  361 us (49%)
  local copies, waits for them, and re-layouts  191 us (26%)
  matrix products  95.3 us (13%)
  other arithmetic  68.4 us (9%)
  between operations  13.5 us (2%)
    all_to_all x1, waiting for transfers between devices, send_pieces(): lax.all_to_all(outgoing, 'tile', split_axis=0, concat_axis=2, tiled=True)  273 us
    reshape x1, local copies, waits for them, and re-layouts, body(): left_basis.reshape(freq_dev, row_tiles, rows_tile, 2, tile_rows, R)  90.5 us
    reduce_scatter x1, waiting for transfers between devices, body(): lax.psum_scatter(jnp.einsum('fpt,tns->fpns', twiddle, traces, preferred_e...  88.6 us
    transpose x1, local copies, waits for them, and re-layouts, body(): jnp.einsum('fqnc,fpqns->cfqps', right_pieces, spectra_pieces, preferred_e...  61.1 us
    dot_general x1, matrix products, body(): jnp.einsum('frtajk,rfajkys->fyrts', left_tiles, operand, preferred_elemen...  40.3 us
    dot_general x1, matrix products, body(): jnp.einsum('fqnc,fpqns->cfqps', right_pieces, spectra_pieces, preferred_e...  33.9 us
    another operation x1, other arithmetic, body(): operand = jnp.stack([upper_half, lower_half], 2)  24.7 us
    dot_general x1, matrix products, body(): jnp.einsum('fpt,tns->fpns', twiddle, traces, preferred_element_type=jnp.f...  21 us
  transfers between devices with their start and end apart: 2, of which 2 were waited for; matrix products, arithmetic and copies ran while one was open for 12% of the time, Pallas kernels for 0%

commit v1 on v0

--- a/solution.py
+++ b/solution.py
@@ -1,13 +1,12 @@
+import functools
 import math
 
 import jax
 import jax.numpy as jnp
 from jax import lax
+from jax.experimental import pallas as pl
+from jax.experimental.pallas import tpu as pltpu
 from jax.sharding import PartitionSpec as P
-
-N = 8192
-TB = 256
-R = 64
 
 
 def twiddles(freq_ids, time_ids, total_time):
@@ -35,14 +34,16 @@
     return jnp.sum(grouped.astype(jnp.float32), axis=3).astype(jnp.bfloat16)
 
 
-def body(traces, right_basis, left_basis, tile_ranks):
+def split_tiles_body(traces, right_basis, left_basis, tile_ranks):
     freq_count = lax.axis_size("freq")
     tile_count = lax.axis_size("tile")
     time_rows, grid_rows, sources = traces.shape
     freq_dev = right_basis.shape[0]
     total_time = time_rows * freq_count
-    tile_rows = N // TB
-    freq_ids = jnp.int32(0) + 1 + jnp.arange(lax.axis_size("freq") * freq_dev, dtype=jnp.int32)
+    tile_rows = tile_ranks.shape[1]
+    rank_max = right_basis.shape[2] // (2 * tile_rows)
+    tile_points = grid_rows * tile_count // tile_rows
+    freq_ids = 1 + jnp.arange(freq_count * freq_dev, dtype=jnp.int32)
     time_ids = lax.axis_index("freq") * time_rows + jnp.arange(time_rows, dtype=jnp.int32)
     twiddle = twiddles(freq_ids, time_ids, total_time)
     spectra = lax.psum_scatter(
@@ -53,15 +54,15 @@
         scatter_dimension=0,
         tiled=True,
     )
-    piece_rows = min(TB, grid_rows)
+    piece_rows = min(tile_points, grid_rows)
     pieces_dev = grid_rows // piece_rows
-    per_tile = max(TB // grid_rows, 1)
+    per_tile = max(tile_points // grid_rows, 1)
     spectra_pieces = spectra.reshape(freq_dev, 2, pieces_dev, piece_rows, sources)
-    right_pieces = right_basis.reshape(freq_dev, pieces_dev, piece_rows, 2 * tile_rows * R)
+    right_pieces = right_basis.reshape(freq_dev, pieces_dev, piece_rows, 2 * tile_rows * rank_max)
     products = jnp.einsum(
         "fqnc,fpqns->cfqps", right_pieces, spectra_pieces, preferred_element_type=jnp.float32
     )
-    products = products.reshape(2, tile_rows, R, freq_dev, pieces_dev, 2, sources)
+    products = products.reshape(2, tile_rows, rank_max, freq_dev, pieces_dev, 2, sources)
     real_part = products[0, :, :, :, :, 0] - products[1, :, :, :, :, 1]
     imag_part = products[0, :, :, :, :, 1] + products[1, :, :, :, :, 0]
     stacked = jnp.transpose(jnp.stack([real_part, imag_part], 0), (1, 3, 4, 0, 2, 5))
@@ -72,7 +73,7 @@
         jnp.int32
     )
     chosen = jnp.sum(tile_ranks[:, :, None, :] * onehot[None, None], axis=-1)
-    keep_rows = jnp.arange(R, dtype=jnp.int32)[None, None, None, :] < chosen[..., None]
+    keep_rows = jnp.arange(rank_max, dtype=jnp.int32)[None, None, None, :] < chosen[..., None]
     keep_rows = jnp.transpose(keep_rows, (1, 0, 2, 3))[:, :, :, None, :, None]
     rank_rows = jnp.where(keep_rows, stacked, jnp.float32(0.0)).astype(jnp.bfloat16)
     coupled = send_pieces(rank_rows, tile_count, tile_rows, per_tile)
@@ -83,11 +84,220 @@
     upper_half = jnp.stack([real_coupled, imag_coupled], -2)
     lower_half = jnp.stack([-imag_coupled, real_coupled], -2)
     operand = jnp.stack([upper_half, lower_half], 2)
-    left_tiles = left_basis.reshape(freq_dev, row_tiles, rows_tile, 2, tile_rows, R)
+    left_tiles = left_basis.reshape(freq_dev, row_tiles, rows_tile, 2, tile_rows, rank_max)
     field_out = jnp.einsum(
         "frtajk,rfajkys->fyrts", left_tiles, operand, preferred_element_type=jnp.float32
     )
     return field_out.reshape(freq_dev, 2, grid_rows, sources).astype(jnp.bfloat16)
+
+
+def pack_kernel(dims, off_ref, rank_ref, me_ref, right_ref, spec_ref, out_ref, own_ref, buf):
+    peers, per_dev, rank, sources, cap, full = dims
+    freq, col = pl.program_id(0), pl.program_id(1)
+    half = peers * per_dev * rank
+    real, imag = spec_ref[0, 0], spec_ref[0, 1]
+    upper = jnp.concatenate([real, imag], axis=1)
+    lower = jnp.concatenate([-imag, real], axis=1)
+    rows = lax.broadcasted_iota(jnp.int32, (rank, 2 * sources), 0)
+    contract = (((0,), (0,)), ((), ()))
+    width = per_dev * rank
+    for peer in range(peers):
+        real_cols = right_ref[0, :, peer * width : (peer + 1) * width]
+        imag_cols = right_ref[0, :, half + peer * width : half + (peer + 1) * width]
+        total = lax.dot_general(real_cols, upper, contract, preferred_element_type=jnp.float32)
+        total += lax.dot_general(imag_cols, lower, contract, preferred_element_type=jnp.float32)
+        for row in range(per_dev):
+            index = ((freq * per_dev + col) * peers + peer) * per_dev + row
+            kept = jnp.where(rows < rank_ref[index], total[row * rank : (row + 1) * rank], 0.0)
+            buf[0, peer, pl.ds(off_ref[index], rank), :] = kept[:, :sources]
+            buf[1, peer, pl.ds(off_ref[index], rank), :] = kept[:, sources:]
+
+    @pl.when((freq == pl.num_programs(0) - 1) & (col == pl.num_programs(1) - 1))
+    def _():
+        @pl.loop(0, peers)
+        def _(peer):
+            for part in range(2):
+                lanes = slice(part * sources, (part + 1) * sources)
+                out_ref[peer, :, lanes] = buf[part, peer, :cap, :].astype(out_ref.dtype)
+
+        for part in range(2):
+            lanes = slice(part * sources, (part + 1) * sources)
+            own_ref[:, lanes] = buf[part, me_ref[0], :full, :].astype(own_ref.dtype)
+
+
+def unpack_kernel(dims, off_ref, rank_ref, me_ref, recv_ref, own_ref, left_ref, out_ref, buf, operand):
+    peers, per_dev, rank, sources, cap, full = dims
+    freq, row = pl.program_id(0), pl.program_id(1)
+    half = peers * per_dev * rank
+
+    @pl.when((freq == 0) & (row == 0))
+    def _():
+        @pl.loop(0, peers)
+        def _(peer):
+            for part in range(2):
+                lanes = slice(part * sources, (part + 1) * sources)
+                buf[part, peer, :cap, :] = recv_ref[peer, :, lanes].astype(jnp.float32)
+
+        for part in range(2):
+            lanes = slice(part * sources, (part + 1) * sources)
+            buf[part, me_ref[0], :full, :] = own_ref[:, lanes].astype(jnp.float32)
+
+    rows = lax.broadcasted_iota(jnp.int32, (rank, sources), 0)
+    for col in range(peers * per_dev):
+        index = (freq * per_dev + row) * (peers * per_dev) + col
+        window = pl.ds(off_ref[index], rank)
+        keep = rows < rank_ref[index]
+        real = jnp.where(keep, buf[0, col // per_dev, window, :], 0.0)
+        imag = jnp.where(keep, buf[1, col // per_dev, window, :], 0.0)
+        upper = slice(col * rank, (col + 1) * rank)
+        lower = slice(half + col * rank, half + (col + 1) * rank)
+        operand[upper, :sources] = real.astype(operand.dtype)
+        operand[upper, sources:] = imag.astype(operand.dtype)
+        operand[lower, :sources] = (-imag).astype(operand.dtype)
+        operand[lower, sources:] = real.astype(operand.dtype)
+    field = jnp.dot(left_ref[0], operand[...], preferred_element_type=jnp.float32)
+    out_ref[0, 0] = field[:, :sources].astype(out_ref.dtype)
+    out_ref[0, 1] = field[:, sources:].astype(out_ref.dtype)
+
+
+def pack(dims, first, count, offsets, ranks, me, right_basis, spectra):
+    peers, per_dev, rank, sources, cap, full = dims
+    points = right_basis.shape[1] // per_dev
+    width = right_basis.shape[2]
+    return pl.pallas_call(
+        functools.partial(pack_kernel, dims),
+        out_shape=(
+            jax.ShapeDtypeStruct((peers, cap, 2 * sources), jnp.bfloat16),
+            jax.ShapeDtypeStruct((full, 2 * sources), jnp.bfloat16),
+        ),
+        grid_spec=pltpu.PrefetchScalarGridSpec(
+            num_scalar_prefetch=3,
+            grid=(count, per_dev),
+            in_specs=[
+                pl.BlockSpec((1, points, width), lambda f, j, *_: (f + first, j, 0)),
+                pl.BlockSpec((1, 2, points, sources), lambda f, j, *_: (f, 0, j, 0)),
+            ],
+            out_specs=[
+                pl.BlockSpec((peers, cap, 2 * sources), lambda f, j, *_: (0, 0, 0)),
+                pl.BlockSpec((full, 2 * sources), lambda f, j, *_: (0, 0)),
+            ],
+            scratch_shapes=[pltpu.VMEM((2, peers, full + rank, sources), jnp.float32)],
+        ),
+        compiler_params=pltpu.CompilerParams(vmem_limit_bytes=62 << 20),
+        cost_estimate=pl.CostEstimate(
+            flops=4 * count * per_dev * points * width * sources,
+            bytes_accessed=2 * count * per_dev * points * width + 4 * peers * cap * sources,
+            transcendentals=0,
+        ),
+        name="pack_rows",
+    )(offsets, ranks, me, right_basis, spectra)
+
+
+def unpack(dims, first, count, offsets, ranks, me, received, own, left_basis):
+    peers, per_dev, rank, sources, cap, full = dims
+    grid_rows, width = left_basis.shape[1:]
+    points = grid_rows // per_dev
+    return pl.pallas_call(
+        functools.partial(unpack_kernel, dims),
+        out_shape=jax.ShapeDtypeStruct((count, 2, grid_rows, sources), jnp.bfloat16),
+        grid_spec=pltpu.PrefetchScalarGridSpec(
+            num_scalar_prefetch=3,
+            grid=(count, per_dev),
+            in_specs=[
+                pl.BlockSpec((peers, cap, 2 * sources), lambda f, i, *_: (0, 0, 0)),
+                pl.BlockSpec((full, 2 * sources), lambda f, i, *_: (0, 0)),
+                pl.BlockSpec((1, points, width), lambda f, i, *_: (f + first, i, 0)),
+            ],
+            out_specs=pl.BlockSpec((1, 2, points, sources), lambda f, i, *_: (f, 0, i, 0)),
+            scratch_shapes=[
+                pltpu.VMEM((2, peers, full + rank, sources), jnp.float32),
+                pltpu.VMEM((width, 2 * sources), jnp.bfloat16),
+            ],
+        ),
+        compiler_params=pltpu.CompilerParams(vmem_limit_bytes=62 << 20),
+        cost_estimate=pl.CostEstimate(
+            flops=4 * count * grid_rows * width * sources,
+            bytes_accessed=2 * count * grid_rows * width + 4 * peers * cap * sources,
+            transcendentals=0,
+        ),
+        name="apply_left",
+    )(offsets, ranks, me, received, own, left_basis)
+
+
+def tile_order(ranks, peers, per_dev):
+    count = ranks.shape[0]
+    split = ranks.reshape(count, peers, per_dev, peers, per_dev)
+    return jnp.transpose(split, (3, 1, 0, 4, 2)).reshape(peers, peers, count * per_dev * per_dev)
+
+
+def pipeline(chunks, packed, traces, right_basis, left_basis, tile_ranks):
+    freq_count = lax.axis_size("freq")
+    peers = lax.axis_size("tile")
+    time_rows, grid_rows, sources = traces.shape
+    freq_dev = right_basis.shape[0]
+    total_time = time_rows * freq_count
+    tile_rows = tile_ranks.shape[1]
+    per_dev = tile_rows // peers
+    rank = right_basis.shape[2] // (2 * tile_rows)
+    time_ids = lax.axis_index("freq") * time_rows + jnp.arange(time_rows, dtype=jnp.int32)
+    me = lax.axis_index("tile").astype(jnp.int32)
+    fields = []
+    for first, count, cap in chunks:
+        freq_ids = (
+            1
+            + jnp.arange(freq_count, dtype=jnp.int32)[:, None] * freq_dev
+            + jnp.arange(first, first + count, dtype=jnp.int32)[None, :]
+        ).reshape(freq_count * count)
+        partial_sums = jnp.einsum(
+            "fpt,tns->fpns",
+            twiddles(freq_ids, time_ids, total_time),
+            traces,
+            preferred_element_type=jnp.float32,
+        ).astype(jnp.bfloat16)
+        spectra = lax.psum_scatter(partial_sums, "freq", scatter_dimension=0, tiled=True)
+        ranks = tile_order(tile_ranks[first : first + count], peers, per_dev)
+        full = count * per_dev * per_dev * rank
+        if packed:
+            offsets = jnp.cumsum(ranks, axis=2) - ranks
+        else:
+            offsets = jnp.broadcast_to(
+                jnp.arange(ranks.shape[2], dtype=jnp.int32) * rank, ranks.shape
+            )
+        dims = (peers, per_dev, rank, sources, cap, full)
+
+        def outgoing(table):
+            mine = lax.dynamic_index_in_dim(table, me, 0, keepdims=False)
+            mine = mine.reshape(peers, count, per_dev, per_dev)
+            return jnp.transpose(mine, (1, 2, 0, 3)).reshape(-1)
+
+        def incoming(table):
+            mine = lax.dynamic_index_in_dim(table, me, 1, keepdims=False)
+            mine = mine.reshape(peers, count, per_dev, per_dev)
+            return jnp.transpose(mine, (1, 3, 0, 2)).reshape(-1)
+
+        sent, own = pack(
+            dims, first, count, outgoing(offsets), outgoing(ranks), me[None], right_basis, spectra
+        )
+        received = lax.all_to_all(sent, "tile", split_axis=0, concat_axis=0, tiled=True)
+        fields.append(
+            unpack(
+                dims, first, count, incoming(offsets), incoming(ranks), me[None], received, own,
+                left_basis,
+            )
+        )
+    return jnp.concatenate(fields, axis=0)
+
+
+def body(traces, right_basis, left_basis, tile_ranks):
+    peers = lax.axis_size("tile")
+    tile_rows = tile_ranks.shape[1]
+    if tile_rows % peers != 0:
+        return split_tiles_body(traces, right_basis, left_basis, tile_ranks)
+    freq_dev = right_basis.shape[0]
+    rank = right_basis.shape[2] // (2 * tile_rows)
+    full = (tile_rows // peers) ** 2 * rank
+    chunks = [(first, 1, full) for first in range(freq_dev)]
+    return pipeline(chunks, False, traces, right_basis, left_basis, tile_ranks)
 
 
 def solution(mesh):

time: 739 us -> 494 us (0.67)
  local copies, waits for them, and re-layouts: 191 us -> 16.9 us
  Pallas kernels: 0 us -> 73.7 us
  other arithmetic: 68.4 us -> 2.8 us
  waiting for transfers between devices: 361 us -> 297 us
  matrix products: 95.3 us -> 61 us
  starting transfers between devices: 5.95 us -> 19.5 us
    unnamed x1 -> x8, waiting for transfers between devices: 0.02 us -> 140 us
    all_to_all x1 -> x4, waiting for transfers between devices: 273 us -> 157 us  [pipeline(): lax.all_to_all(sent, 'tile', split_axis=0, concat_axis=0, tiled=True)]
    reduce_scatter x1 -> x0, waiting for transfers between devices: 88.6 us -> none  [body(): lax.psum_scatter(jnp.einsum('fpt,tns->fpns', twiddle, traces, preferred_e...]
    reshape x1 -> x13, local copies, waits for them, and re-layouts: 90.5 us -> 6.04 us  [the longest x5 3.25 us: incoming(): return jnp.transpose(mine, (1, 3, 0, 2)).reshape(-1)]
    pallas_call x0 -> x8, Pallas kernels: none -> 73.7 us  [the longest x4 37.7 us: pack(): pl.pallas_call(functools.partial(pack_kernel, dims), out_shape=(jax.Shape...]
    transpose x1 -> x15, local copies, waits for them, and re-layouts: 61.1 us -> 2.66 us  [the longest x4 1.23 us: tile_order(): jnp.transpose(split, (3, 1, 0, 4, 2))]
    dot_general x3 -> x4, matrix products: 95.3 us -> 61 us  [pipeline(): jnp.einsum('fpt,tns->fpns', twiddles(freq_ids, time_ids, total_time), tra...]
    another operation x2 -> x1, other arithmetic: 24.8 us -> 0.16 us  [the longest x1 24.7 us: body(): operand = jnp.stack([upper_half, lower_half], 2)]
  transfers between devices with their start and end apart: 2 -> 8, of which waited for: 2 -> 8; matrix products, arithmetic and copies ran while one was open for 12% -> 13% of each run, Pallas kernels for 0% -> 11%
where the time goes in v1:
time: 494 us; the launch traced here: 485 us
  waiting for transfers between devices  297 us (60%)
  Pallas kernels  73.7 us (15%)
  matrix products  61 us (12%)
  starting transfers between devices  19.5 us (4%)
  local copies, waits for them, and re-layouts  16.9 us (3%)
  between operations  13.7 us (3%)
    all_to_all x4, waiting for transfers between devices, pipeline(): lax.all_to_all(sent, 'tile', split_axis=0, concat_axis=0, tiled=True)  157 us
    unnamed x8, waiting for transfers between devices  140 us
    dot_general x4, matrix products, pipeline(): jnp.einsum('fpt,tns->fpns', twiddles(freq_ids, time_ids, total_time), tra...  61 us
    pallas_call x4, Pallas kernels, pack(): pl.pallas_call(functools.partial(pack_kernel, dims), out_shape=(jax.Shape...  37.7 us
    pallas_call x4, Pallas kernels, unpack(): pl.pallas_call(functools.partial(unpack_kernel, dims), out_shape=jax.Shap...  36 us
    all_to_all x4, starting transfers between devices, pipeline(): lax.all_to_all(sent, 'tile', split_axis=0, concat_axis=0, tiled=True)  19 us
  transfers between devices with their start and end apart: 8, of which 8 were waited for; matrix products, arithmetic and copies ran while one was open for 13% of the time, Pallas kernels for 11%

profile of v1, /device:TPU:0, one launch (start us, length us, event | category | flops | bytes accessed | tf_op | source)
XLA Modules:
  0.0 485.0 jit_solution(9365282886422052632)
XLA Ops:
  6.7 15.3 %fusion.21 = bf16[4,2,1024,128]{3,0,2,1:T(4,128)(2,1)S(1)} fusion(bf16[64,1024,128]{2,1,0:T(8,128)(2,1)} %param.4, bf16[4,1,64]{2,0,1:T(4,128)(2,1)S(1)} %get-tuple-element.37, bf16[4,1,64]{2,0,1:T(4,128)(2,1)S(1)} %get-tuple-element.38), kind=kOutput, calls=%fused_computation.16 | convolution fusion | flops 135268352 | bytes 18875392 | tf_op jit(solution)/shard_map/fpt,tns->fpns/dot_general | solution.py:251
  22.0 1.7 copy.113
  25.4 36.3 %reduce-scatter.19.cloned.1.call-done.spec_ref = bf16[1,2,1024,128]{3,2,1,0:T(8,128)(2,1)} async-done(((bf16[4,2,1024,128]{3,2,1,0:T(8,128)(2,1)}), bf16[1,2,1024,128]{3,2,1,0:T(8,128)(2,1)}) %reduce-scatter.19.cloned.1.call-update) | async-done | bytes 524304
  61.7 9.5 %pack_rows.7 = (bf16[8,1024,256]{2,1,0:T(8,128)(2,1)}, bf16[1024,256]{1,0:T(8,128)(2,1)}) custom-call(s32[128]{0:T(128)} %transpose.71.off_ref, s32[128]{0:T(128)} %reshape.668.rank_ref, s32[1]{0:T(128)} %bitcast.4.me_ref, bf16[4,1024,4096]{2,1,0:T(8,128)(2,1)} %right_ref.7, bf16[1,2,1024,128]{3,2,1,0:T(8,128)(2,1)} %reduce-scatter.19.cloned.1.call-done.spec_ref), custom_call_target="tpu_custom_call" | custom-call | flops 2147483648 | bytes 12582912 | tf_op jit(solution)/shard_map/pack_rows/pallas_call | solution.py:167
  71.2 5.0 %all-to-all-start.3 = ((bf16[8,1024,256]{2,1,0:T(8,128)(2,1)}), bf16[8,1024,256]{2,1,0:T(8,128)(2,1)}, u32[]{:S(2)}, u32[]{:S(2)}) async-start(bf16[8,1024,256]{2,1,0:T(8,128)(2,1)} %get-tuple-element.19), calls=%async_computation.3 | async-start | bytes 8388608 | tf_op jit(solution)/shard_map/all_to_all | solution.py:281
  76.3 15.3 %fusion.18 = bf16[4,2,1024,128]{3,0,2,1:T(4,128)(2,1)S(1)} fusion(bf16[64,1024,128]{2,1,0:T(8,128)(2,1)} %param.4, bf16[4,1,64]{2,0,1:T(4,128)(2,1)S(1)} %get-tuple-element.33, bf16[4,1,64]{2,0,1:T(4,128)(2,1)S(1)} %get-tuple-element.34), kind=kOutput, calls=%fused_computation.15 | convolution fusion | flops 135268352 | bytes 18875392 | tf_op jit(solution)/shard_map/fpt,tns->fpns/dot_general | solution.py:251
  91.6 1.7 copy.108
  94.4 34.6 %reduce-scatter.17.cloned.1.call-done.spec_ref = bf16[1,2,1024,128]{3,2,1,0:T(8,128)(2,1)} async-done(((bf16[4,2,1024,128]{3,2,1,0:T(8,128)(2,1)}), bf16[1,2,1024,128]{3,2,1,0:T(8,128)(2,1)}) %reduce-scatter.17.cloned.1.call-update) | async-done | bytes 524304
  129.0 9.4 %pack_rows.6 = (bf16[8,1024,256]{2,1,0:T(8,128)(2,1)}, bf16[1024,256]{1,0:T(8,128)(2,1)}) custom-call(s32[128]{0:T(128)} %transpose.71.off_ref, s32[128]{0:T(128)} %reshape.662.rank_ref, s32[1]{0:T(128)} %bitcast.4.me_ref, bf16[4,1024,4096]{2,1,0:T(8,128)(2,1)} %right_ref.7, bf16[1,2,1024,128]{3,2,1,0:T(8,128)(2,1)} %reduce-scatter.17.cloned.1.call-done.spec_ref), custom_call_target="tpu_custom_call" | custom-call | flops 2147483648 | bytes 12582912 | tf_op jit(solution)/shard_map/pack_rows/pallas_call | solution.py:167
  138.4 31.9 %all-to-all-done.3.recv_ref = bf16[8,1024,256]{2,1,0:T(8,128)(2,1)} async-done(((bf16[8,1024,256]{2,1,0:T(8,128)(2,1)}), bf16[8,1024,256]{2,1,0:T(8,128)(2,1)}, u32[]{:S(2)}, u32[]{:S(2)}) %all-to-all-start.3) | async-done | bytes 4194336 | tf_op jit(solution)/shard_map/all_to_all | solution.py:281
  170.3 4.6 all-to-all-start.2
  175.1 15.3 %fusion.15 = bf16[4,2,1024,128]{3,0,2,1:T(4,128)(2,1)S(1)} fusion(bf16[64,1024,128]{2,1,0:T(8,128)(2,1)} %param.4, bf16[4,1,64]{2,0,1:T(4,128)(2,1)S(1)} %get-tuple-element.35, bf16[4,1,64]{2,0,1:T(4,128)(2,1)S(1)} %get-tuple-element.36), kind=kOutput, calls=%fused_computation.14 | convolution fusion | flops 135268352 | bytes 18875392 | tf_op jit(solution)/shard_map/fpt,tns->fpns/dot_general | solution.py:251
  190.4 1.7 copy.103
  193.2 34.5 %reduce-scatter.15.cloned.1.call-done.spec_ref = bf16[1,2,1024,128]{3,2,1,0:T(8,128)(2,1)} async-done(((bf16[4,2,1024,128]{3,2,1,0:T(8,128)(2,1)}), bf16[1,2,1024,128]{3,2,1,0:T(8,128)(2,1)}) %reduce-scatter.15.cloned.1.call-update) | async-done | bytes 524304
  227.8 9.4 %pack_rows.5 = (bf16[8,1024,256]{2,1,0:T(8,128)(2,1)}, bf16[1024,256]{1,0:T(8,128)(2,1)}) custom-call(s32[128]{0:T(128)} %transpose.71.off_ref, s32[128]{0:T(128)} %reshape.656.rank_ref, s32[1]{0:T(128)} %bitcast.4.me_ref, bf16[4,1024,4096]{2,1,0:T(8,128)(2,1)} %right_ref.7, bf16[1,2,1024,128]{3,2,1,0:T(8,128)(2,1)} %reduce-scatter.15.cloned.1.call-done.spec_ref), custom_call_target="tpu_custom_call" | custom-call | flops 2147483648 | bytes 12582912 | tf_op jit(solution)/shard_map/pack_rows/pallas_call | solution.py:167
  237.2 31.7 %all-to-all-done.2.recv_ref = bf16[8,1024,256]{2,1,0:T(8,128)(2,1)} async-done(((bf16[8,1024,256]{2,1,0:T(8,128)(2,1)}), bf16[8,1024,256]{2,1,0:T(8,128)(2,1)}, u32[]{:S(2)}, u32[]{:S(2)}) %all-to-all-start.2) | async-done | bytes 4194336 | tf_op jit(solution)/shard_map/all_to_all | solution.py:281
  268.9 4.6 all-to-all-start.1
  273.7 15.3 %fusion.12 = bf16[4,2,1024,128]{3,0,2,1:T(4,128)(2,1)S(1)} fusion(bf16[64,1024,128]{2,1,0:T(8,128)(2,1)} %param.4, bf16[4,1,64]{2,0,1:T(4,128)(2,1)S(1)} %get-tuple-element.26, bf16[4,1,64]{2,0,1:T(4,128)(2,1)S(1)} %get-tuple-element.25), kind=kOutput, calls=%fused_computation.13 | convolution fusion | flops 135268352 | bytes 18875392 | tf_op jit(solution)/shard_map/fpt,tns->fpns/dot_general | solution.py:251
  289.0 1.7 copy.98
  291.8 34.6 %reduce-scatter.13.cloned.1.call-done.spec_ref = bf16[1,2,1024,128]{3,2,1,0:T(8,128)(2,1)} async-done(((bf16[4,2,1024,128]{3,2,1,0:T(8,128)(2,1)}), bf16[1,2,1024,128]{3,2,1,0:T(8,128)(2,1)}) %reduce-scatter.13.cloned.1.call-update) | async-done | bytes 524304
  326.4 9.4 %pack_rows.4 = (bf16[8,1024,256]{2,1,0:T(8,128)(2,1)}, bf16[1024,256]{1,0:T(8,128)(2,1)}) custom-call(s32[128]{0:T(128)} %transpose.71.off_ref, s32[128]{0:T(128)} %reshape.650.rank_ref, s32[1]{0:T(128)} %bitcast.4.me_ref, bf16[4,1024,4096]{2,1,0:T(8,128)(2,1)} %right_ref.7, bf16[1,2,1024,128]{3,2,1,0:T(8,128)(2,1)} %reduce-scatter.13.cloned.1.call-done.spec_ref), custom_call_target="tpu_custom_call" | custom-call | flops 2147483648 | bytes 12582912 | tf_op jit(solution)/shard_map/pack_rows/pallas_call | solution.py:167
  335.8 31.7 %all-to-all-done.1.recv_ref = bf16[8,1024,256]{2,1,0:T(8,128)(2,1)} async-done(((bf16[8,1024,256]{2,1,0:T(8,128)(2,1)}), bf16[8,1024,256]{2,1,0:T(8,128)(2,1)}, u32[]{:S(2)}, u32[]{:S(2)}) %all-to-all-start.1) | async-done | bytes 4194336 | tf_op jit(solution)/shard_map/all_to_all | solution.py:281
  367.5 4.8 all-to-all-start
  373.0 0.7 dynamic-slice_reduce_fusion
  373.8 0.7 reshape.666.rank_ref
  375.2 0.7 dynamic-slice_reduce_fusion.2
  377.4 9.0 %apply_left.7 = bf16[1,2,1024,128]{3,2,1,0:T(8,128)(2,1)} custom-call(s32[128]{0:T(128)} %reshape.644.off_ref, s32[128]{0:T(128)} %reshape.666.rank_ref, s32[1]{0:T(128)} %bitcast.4.me_ref, bf16[8,1024,256]{2,1,0:T(8,128)(2,1)} %all-to-all-done.3.recv_ref, bf16[1024,256]{1,0:T(8,128)(2,1)} %get-tuple-element.20.own_ref, bf16[4,1024,4096]{2,1,0:T(8,128)(2,1)} %left_ref.7), custom_call_target="tpu_custom_call" | custom-call | flops 2147483648 | bytes 12582912 | tf_op jit(solution)/shard_map/apply_left/pallas_call | solution.py:200
  386.4 9.0 %apply_left.6 = bf16[1,2,1024,128]{3,2,1,0:T(8,128)(2,1)} custom-call(s32[128]{0:T(128)} %reshape.644.off_ref, s32[128]{0:T(128)} %reshape.660.rank_ref, s32[1]{0:T(128)} %bitcast.4.me_ref, bf16[8,1024,256]{2,1,0:T(8,128)(2,1)} %all-to-all-done.2.recv_ref, bf16[1024,256]{1,0:T(8,128)(2,1)} %get-tuple-element.18.own_ref, bf16[4,1024,4096]{2,1,0:T(8,128)(2,1)} %left_ref.7), custom_call_target="tpu_custom_call" | custom-call | flops 2147483648 | bytes 12582912 | tf_op jit(solution)/shard_map/apply_left/pallas_call | solution.py:200
  395.3 9.0 %apply_left.5 = bf16[1,2,1024,128]{3,2,1,0:T(8,128)(2,1)} custom-call(s32[128]{0:T(128)} %reshape.644.off_ref, s32[128]{0:T(128)} %reshape.654.rank_ref, s32[1]{0:T(128)} %bitcast.4.me_ref, bf16[8,1024,256]{2,1,0:T(8,128)(2,1)} %all-to-all-done.1.recv_ref, bf16[1024,256]{1,0:T(8,128)(2,1)} %get-tuple-element.16.own_ref, bf16[4,1024,4096]{2,1,0:T(8,128)(2,1)} %left_ref.7), custom_call_target="tpu_custom_call" | custom-call | flops 2147483648 | bytes 12582912 | tf_op jit(solution)/shard_map/apply_left/pallas_call | solution.py:200
  404.3 62.0 %all-to-all-done.recv_ref = bf16[8,1024,256]{2,1,0:T(8,128)(2,1)} async-done(((bf16[8,1024,256]{2,1,0:T(8,128)(2,1)}), bf16[8,1024,256]{2,1,0:T(8,128)(2,1)}, u32[]{:S(2)}, u32[]{:S(2)}) %all-to-all-start) | async-done | bytes 4194336 | tf_op jit(solution)/shard_map/all_to_all | solution.py:281
  466.3 9.1 %apply_left.4 = bf16[1,2,1024,128]{3,2,1,0:T(8,128)(2,1)} custom-call(s32[128]{0:T(128)} %reshape.644.off_ref, s32[128]{0:T(128)} %reshape.648.rank_ref, s32[1]{0:T(128)} %bitcast.4.me_ref, bf16[8,1024,256]{2,1,0:T(8,128)(2,1)} %all-to-all-done.recv_ref, bf16[1024,256]{1,0:T(8,128)(2,1)} %get-tuple-element.14.own_ref, bf16[4,1024,4096]{2,1,0:T(8,128)(2,1)} %left_ref.7), custom_call_target="tpu_custom_call" | custom-call | flops 2147483648 | bytes 12582912 | tf_op jit(solution)/shard_map/apply_left/pallas_call | solution.py:200
  475.4 2.6 pad_maximum_fusion
  (54 shorter events, 8.9 us)
Async XLA Ops:
  6.5 55.2 %reduce-scatter.19.cloned.1.call-start = ((), (), s32[]{:S(2)}) async-start(), calls=%async_computation.11 | async-start | bytes 2621440
  22.0 1.7 copy-start.3
  71.2 99.1 %all-to-all-start.3 = ((bf16[8,1024,256]{2,1,0:T(8,128)(2,1)}), bf16[8,1024,256]{2,1,0:T(8,128)(2,1)}, u32[]{:S(2)}, u32[]{:S(2)}) async-start(bf16[8,1024,256]{2,1,0:T(8,128)(2,1)} %get-tuple-element.19), calls=%async_computation.3 | async-start | bytes 8388608 | tf_op jit(solution)/shard_map/all_to_all | solution.py:281
  76.3 52.8 %reduce-scatter.17.cloned.1.call-start = ((), (), s32[]{:S(2)}) async-start(), calls=%async_computation.10 | async-start | bytes 2621440
  170.3 98.5 %all-to-all-start.2 = ((bf16[8,1024,256]{2,1,0:T(8,128)(2,1)}), bf16[8,1024,256]{2,1,0:T(8,128)(2,1)}, u32[]{:S(2)}, u32[]{:S(2)}) async-start(bf16[8,1024,256]{2,1,0:T(8,128)(2,1)} %get-tuple-element.17), calls=%async_computation.2 | async-start | bytes 8388608 | tf_op jit(solution)/shard_map/all_to_all | solution.py:281
  174.9 52.9 %reduce-scatter.15.cloned.1.call-start = ((), (), s32[]{:S(2)}) async-start(), calls=%async_computation.9 | async-start | bytes 2621440
  268.9 98.6 %all-to-all-start.1 = ((bf16[8,1024,256]{2,1,0:T(8,128)(2,1)}), bf16[8,1024,256]{2,1,0:T(8,128)(2,1)}, u32[]{:S(2)}, u32[]{:S(2)}) async-start(bf16[8,1024,256]{2,1,0:T(8,128)(2,1)} %get-tuple-element.15), calls=%async_computation.1 | async-start | bytes 8388608 | tf_op jit(solution)/shard_map/all_to_all | solution.py:281
  273.5 52.9 %reduce-scatter.13.cloned.1.call-start = ((), (), s32[]{:S(2)}) async-start(), calls=%async_computation.8 | async-start | bytes 2621440
  367.5 98.8 %all-to-all-start = ((bf16[8,1024,256]{2,1,0:T(8,128)(2,1)}), bf16[8,1024,256]{2,1,0:T(8,128)(2,1)}, u32[]{:S(2)}, u32[]{:S(2)}) async-start(bf16[8,1024,256]{2,1,0:T(8,128)(2,1)} %get-tuple-element.13), calls=%async_computation | async-start | bytes 8388608 | tf_op jit(solution)/shard_map/all_to_all | solution.py:281
  466.3 9.1 %copy-start = (bf16[1,2,1024,128]{3,2,1,0:T(8,128)(2,1)S(1)}, bf16[1,2,1024,128]{3,2,1,0:T(8,128)(2,1)}, u32[]{:S(2)}) copy-start(bf16[1,2,1024,128]{3,2,1,0:T(8,128)(2,1)} %apply_left.7) | copy-start | bytes 1572868
  466.3 9.1 %copy-start.1 = (bf16[1,2,1024,128]{3,2,1,0:T(8,128)(2,1)S(1)}, bf16[1,2,1024,128]{3,2,1,0:T(8,128)(2,1)}, u32[]{:S(2)}) copy-start(bf16[1,2,1024,128]{3,2,1,0:T(8,128)(2,1)} %apply_left.6) | copy-start | bytes 1572868
  466.3 9.1 %copy-start.2 = (bf16[1,2,1024,128]{3,2,1,0:T(8,128)(2,1)S(1)}, bf16[1,2,1024,128]{3,2,1,0:T(8,128)(2,1)}, u32[]{:S(2)}) copy-start(bf16[1,2,1024,128]{3,2,1,0:T(8,128)(2,1)} %apply_left.5) | copy-start | bytes 1572868
Sparse Core Ops, SparseCore 0:
  23.8 37.9 reduce-scatter.18
  93.4 35.6 reduce-scatter.16
  192.2 35.5 reduce-scatter.14
  290.8 35.5 reduce-scatter.12
